TPU v7x, 1024 devices: a whole 4x4x32 slice. The times are simulated.
1024 devices in a mesh: dp: 32 (over z), pipe: 8 (over x, core), tensor: 4 (over y).
Axes of the slice: x: 4, y: 4, z: 32, core: 2. Of those that a mesh axis runs over, the one named last changes fastest.
Arguments:
- residual: bfloat16 [8, 2, 2048, 6144], P('pipe', None, 'dp', 'tensor'), may hold values from -6 to 6
- queries: bfloat16 [8, 2, 2048, 6144], P('pipe', None, 'dp', 'tensor'), may hold values from -6 to 6
- keys_values: bfloat16 [8, 2, 2, 2048, 6144], P('pipe', None, None, 'dp', 'tensor'), may hold values from -18 to 18
- global_kv: bfloat16 [8, 2, 2, 384, 6144], P('pipe', None, None, None, 'tensor'), may hold values from -6 to 6
- block_ids: int32 [8, 2, 32, 48], P('pipe', None, 'dp', 'tensor'), may hold values from 0 to 31, as said below
- lengths: int32 [8, 2], P('pipe'), may hold values from 8 to 32, as said below
- gain: bfloat16 [8, 2, 6144], P('pipe', None, 'tensor'), may hold values from 0.5 to 1.5
Outputs:
- normed: bfloat16 [8, 2, 2048, 6144], P('pipe', None, 'dp', 'tensor')
Inputs may be any that keep to these rules, and one draw needn't show every extreme that they name: `block_ids`: for one section and direction, the random blocks of the 1 query block of one index of dp in the 12 heads of one index of tensor lie at most 1 in the 1 block of any one index of dp, and exactly 1 for some index. `lengths`: for each section one of the two micro-batches has all 32 blocks live.
All inputs are finite; a program needn't handle non-finite values.
Results may differ from a plain program's by a relative error of at most 0.0053.
Values may be sent and summed in bfloat16 or wider, within the bound.
A program may use at most 64 MiB of HBM per device.

v0:
```python
import jax
import jax.numpy as jnp
from jax import lax
from jax.sharding import PartitionSpec as P

D = 6144
HD = 128
BLK = 64


epsilon = 1e-05


def padded_2(array, sides, width):
    for axis, dim in sides:
        peers, length = (lax.axis_size(axis), array.shape[dim])
        up = [(i, (i + 1) % peers) for i in range(peers - 1)]
        down = [(j, i) for i, j in up]
        last = lax.slice_in_dim(array, length - width, length, axis=dim)
        leading = lax.slice_in_dim(array, 0, width, axis=dim)
        before = lax.ppermute(last, axis, up)
        after = lax.ppermute(leading, axis, down)
        array = jnp.concatenate([before, array, after], axis=dim)
    return array


def request_slots(block_index, blocks_dev, capacity):
    owner_dev = block_index // blocks_dev
    local_block = block_index % blocks_dev
    count = block_index.shape[-1]
    request_order = jnp.arange(count, dtype=jnp.int32)
    same_owner = (owner_dev[:, :, None] == owner_dev[:, None, :]) & (
        request_order[None, None, :] < request_order[None, :, None]
    )
    slot_rank = jnp.sum(same_owner.astype(jnp.int32), axis=2)
    direction = jnp.arange(2, dtype=jnp.int32)[:, None]
    position = owner_dev * (2 * capacity) + direction * capacity + slot_rank
    return (owner_dev, local_block, position)


def send_tiles(tiles):
    return lax.all_to_all(tiles, "dp", split_axis=0, concat_axis=0, tiled=True)


def body(residual, queries, keys_values, global_kv, block_ids, lengths, gain):
    width_dev = residual.shape[-1]
    head_count = width_dev // HD
    tok_rows = residual.shape[2]
    blocks_dev = tok_rows // BLK
    glob_count = global_kv.shape[3]
    dp_count = lax.axis_size("dp")
    myself = lax.axis_index("dp")
    requests = blocks_dev * head_count
    capacity = (requests + dp_count - 1) // dp_count
    slot_count = 2 * capacity
    padded = padded_2(keys_values, (("dp", 3),), BLK)[0]
    views = [
        padded[:, :, offset * BLK : offset * BLK + tok_rows].reshape(
            2, 2, blocks_dev, BLK, width_dev
        )
        for offset in range(3)
    ]
    window = jnp.stack(views, axis=3).reshape(2, 2, blocks_dev, 3 * BLK, head_count, HD)
    own_pair = keys_values[0].reshape(2, 2, blocks_dev, BLK, head_count, HD)
    tile_table = own_pair.transpose(1, 2, 4, 0, 3, 5).reshape(
        2 * blocks_dev * head_count, 2, BLK, HD
    )
    block_index = block_ids[0].reshape(2, requests)
    head_of = jnp.arange(requests, dtype=jnp.int32) % head_count
    owner_dev, local_block, position = request_slots(block_index, blocks_dev, capacity)
    tile_code = (
        jnp.arange(2, dtype=jnp.int32)[:, None] * blocks_dev + local_block
    ) * head_count + head_of[None, :]
    matches = (
        position.reshape(-1)[None, :] == jnp.arange(dp_count * slot_count, dtype=jnp.int32)[:, None]
    )
    wanted = jnp.sum(jnp.where(matches, tile_code.reshape(-1)[None, :], 0), axis=1).reshape(
        dp_count, slot_count
    )
    received = send_tiles(
        tile_table[lax.all_to_all(wanted, "dp", split_axis=0, concat_axis=0, tiled=True)]
    )
    picked = received.reshape(dp_count * slot_count, 2, BLK, HD)[position.reshape(-1)]
    random_pair = picked.reshape(2, blocks_dev, head_count, 2, BLK, HD)
    query_blocks = queries[0].reshape(2, blocks_dev, BLK, head_count, HD)
    global_pair = global_kv[0].reshape(2, 2, glob_count, head_count, HD)
    window_scores = jnp.einsum(
        "dqbhe,dqkhe->dqhbk", query_blocks, window[0], preferred_element_type=jnp.float32
    )
    global_scores = jnp.einsum(
        "dqbhe,dkhe->dqhbk", query_blocks, global_pair[0], preferred_element_type=jnp.float32
    )
    random_scores = jnp.einsum(
        "dqbhe,dqhke->dqhbk",
        query_blocks,
        random_pair[:, :, :, 0],
        preferred_element_type=jnp.float32,
    )
    scores = jnp.concatenate([window_scores, global_scores, random_scores], axis=4) * HD ** (-0.5)
    seq_blocks = lengths[0]
    query_index = myself * blocks_dev + jnp.arange(blocks_dev, dtype=jnp.int32)
    near_index = query_index[:, None] + jnp.arange(3, dtype=jnp.int32)[None, :] - 1
    near_valid = (near_index[None] >= 0) & (near_index[None] < seq_blocks[:, None, None])
    near_valid = jnp.repeat(near_valid, BLK, axis=2)[:, :, None, None, :]
    random_valid = (block_ids[0] < seq_blocks[:, None, None])[:, :, :, None, None]
    key_valid = jnp.concatenate(
        [
            jnp.broadcast_to(near_valid, (2, blocks_dev, head_count, 1, 3 * BLK)),
            jnp.ones((2, blocks_dev, head_count, 1, glob_count), jnp.bool_),
            jnp.broadcast_to(random_valid, (2, blocks_dev, head_count, 1, BLK)),
        ],
        axis=4,
    )
    scores = jnp.where(key_valid, scores, -jnp.inf)
    largest = jnp.max(scores, axis=4, keepdims=True)
    weights = jnp.exp(scores - largest)
    weights = (weights / jnp.sum(weights, axis=4, keepdims=True)).astype(jnp.bfloat16)
    near_end = 3 * BLK
    glob_end = near_end + glob_count
    context = jnp.einsum(
        "dqhbk,dqkhe->dqbhe", weights[..., :near_end], window[1], preferred_element_type=jnp.float32
    )
    context = context + jnp.einsum(
        "dqhbk,dkhe->dqbhe",
        weights[..., near_end:glob_end],
        global_pair[1],
        preferred_element_type=jnp.float32,
    )
    context = context + jnp.einsum(
        "dqhbk,dqhke->dqbhe",
        weights[..., glob_end:],
        random_pair[:, :, :, 1],
        preferred_element_type=jnp.float32,
    )
    query_valid = (query_index[None, :] < seq_blocks[:, None])[:, :, None, None, None]
    context = jnp.where(query_valid, context, 0.0).reshape(2, tok_rows, width_dev)
    updated = (residual[0].astype(jnp.float32) + context).astype(jnp.bfloat16)
    neighbours = padded_2(updated[None], (("pipe", 1),), 1)[0]
    arrived = jnp.stack([neighbours[3], neighbours[0]], axis=0)
    wide = arrived.astype(jnp.float32)
    squares = lax.psum(jnp.sum(wide * wide, axis=2), "tensor")
    inverse = lax.rsqrt(squares / D + epsilon)
    normed = (wide * inverse[:, :, None] * gain[0][:, None, :].astype(jnp.float32)).astype(
        jnp.bfloat16
    )
    return normed[None]


def solution(mesh):
    in_specs = (
        P("pipe", None, "dp", "tensor"),
        P("pipe", None, "dp", "tensor"),
        P("pipe", None, None, "dp", "tensor"),
        P("pipe", None, None, None, "tensor"),
        P("pipe", None, "dp", "tensor"),
        P("pipe", None),
        P("pipe", None, "tensor"),
    )
    out_specs = P("pipe", None, "dp", "tensor")
    return jax.shard_map(body, mesh=mesh, in_specs=in_specs, out_specs=out_specs, check_vma=False)
```

profile of v0, /device:TPU:1, one launch (start us, length us, event | category | flops | bytes accessed | tf_op | source)
XLA Modules:
  0.0 313.5 jit_solution(11147430903197307491)
XLA Ops:
  0.0 0.7 broadcast_multiply_fusion
  0.7 0.8 copy.54
  1.5 1.0 fusion.10
  3.0 0.7 all_to_all.11
  3.8 29.3 %all-to-all-start = ((s32[32,1,2]{2,1,0:T(1,128)}), s32[32,1,2]{2,1,0:T(1,128)S(1)}, u32[]{:S(2)}, u32[]{:S(2)}) async-start(s32[32,1,2]{2,1,0:T(1,128)} %bitcast.14), calls=%async_computation | async-start | bytes 32768 | tf_op jit(solution)/shard_map/all_to_all | solution.py:81
  33.0 1.6 reshape_squeeze.2
  34.7 0.2 copy.53
  34.9 19.3 %all-to-all-done = s32[32,1,2]{2,1,0:T(1,128)S(1)} async-done(((s32[32,1,2]{2,1,0:T(1,128)}), s32[32,1,2]{2,1,0:T(1,128)S(1)}, u32[]{:S(2)}, u32[]{:S(2)}) %all-to-all-start) | async-done | bytes 288 | tf_op jit(solution)/shard_map/all_to_all | solution.py:81
  54.4 0.1 reshape.457
  54.5 2.1 gather_fusion
  56.6 4.9 %all-to-all-start.1 = ((bf16[32,2,2,64,128]{4,3,2,1,0:T(8,128)(2,1)}), bf16[32,2,2,64,128]{4,3,2,1,0:T(8,128)(2,1)}, u32[]{:S(2)}, u32[]{:S(2)}) async-start(bf16[32,2,2,64,128]{4,3,2,1,0:T(8,128)(2,1)} %bitcast.16), calls=%async_computation.1 | async-start | bytes 4194304 | tf_op jit(solution)/shard_map/all_to_all | solution.py:42
  61.5 1.3 collective-permute-start.1
  62.8 4.9 %collective-permute-start = (bf16[1,2,2,64,1536]{4,3,2,1,0:T(8,128)(2,1)}, bf16[1,2,2,64,1536]{4,3,2,1,0:T(8,128)(2,1)}, u32[]{:S(2)}, u32[]{:S(2)}) collective-permute-start(bf16[1,2,2,64,1536]{4,3,2,1,0:T(8,128)(2,1)} %param.9), channel_id=1, source_target_pairs={{0,32},{32,64},{64,96},{96,128},{128,160},{160,192},{192,224},{224... | collective-permute-start | bytes 2359304 | tf_op jit(solution)/shard_map/ppermute | solution.py:21
  68.0 0.3 reshape.444
  68.3 4.2 %fusion.14 = (bf16[1,1,2,384,1536]{4,3,2,1,0:T(8,128)(2,1)S(1)}, bf16[1,1,2,384,1536]{4,3,2,1,0:T(8,128)(2,1)}) fusion(bf16[1,2,2,384,1536]{4,3,2,1,0:T(8,128)(2,1)} %param.10), kind=kLoop, calls=%fused_computation.57 | loop fusion | bytes 9437184 | tf_op jit(solution)/shard_map/slice | solution.py:126
  72.5 4.3 %copy.68 = bf16[1,1,2,384,1536]{3,4,2,1,0:T(8,128)(2,1)} copy(bf16[1,1,2,384,1536]{4,3,2,1,0:T(8,128)(2,1)} %get-tuple-element.6) | data formatting | bytes 4718592
  77.1 2.4 copy.69
  79.9 2.2 convolution_bitcast_fusion
  82.1 177.5 %collective-permute-done.1 = bf16[1,2,2,64,1536]{4,3,2,1,0:T(8,128)(2,1)} collective-permute-done((bf16[1,2,2,64,1536]{4,3,2,1,0:T(8,128)(2,1)}, bf16[1,2,2,64,1536]{4,3,2,1,0:T(8,128)(2,1)}, u32[]{:S(2)}, u32[]{:S(2)}) %collective-permute-start.1) | collective-permute-done | bytes 786464 | tf_op jit(solution)/shard_map/ppermute | solution.py:22
  259.6 1.8 maximum_bitcast_fusion
  261.4 0.2 slice_bitcast_fusion.6
  261.5 0.3 pad_maximum_fusion
  261.8 1.2 fusion.15
  263.0 1.1 copy.47
  264.1 3.5 %reshape.443 = bf16[2,192,12,128]{3,2,1,0:T(8,128)(2,1)} reshape(bf16[1,2,1,3,64,1536]{5,4,3,1,2,0:T(8,128)(2,1)} %copy.47) | data formatting | bytes 2359296 | tf_op jit(solution)/shard_map/reshape.23
  267.6 2.4 copy.46
  270.0 3.4 %reshape.442 = bf16[2,192,12,128]{3,2,1,0:T(8,128)(2,1)} reshape(bf16[1,2,1,3,64,1536]{5,4,3,1,2,0:T(8,128)(2,1)} %copy.46) | data formatting | bytes 2359296 | tf_op jit(solution)/shard_map/reshape.36
  273.4 3.4 %convolution_bitcast_fusion.1 = f32[2,1,12,64,192]{4,3,2,0,1:T(8,128)} fusion(bf16[2,192,12,128]{3,2,1,0:T(8,128)(2,1)} %reshape.443, bf16[2,64,12,128]{3,2,1,0:T(8,128)(2,1)S(1)} %reshape.444), kind=kOutput, calls=%fused_computation.10 | convolution fusion | flops 75497472 | bytes 2752512 | tf_op jit(solution)/shard_map/dqbhe,dqkhe->dqhbk/dot_general | solution.py:87
  276.8 3.2 %gather_fusion.1 = bf16[24,2,64,128]{3,2,1,0:T(8,128)(2,1)} fusion(bf16[64,2,64,128]{3,2,1,0:T(8,128)(2,1)} %bitcast.17, s32[1024]{0:T(1024)S(1)} %pad_clamp_fusion), kind=kCustom, calls=%fused_computation.1 | custom fusion | bytes 1572960 | tf_op jit(solution)/shard_map/gather | solution.py:83
  280.1 1.3 copy.60
  281.4 0.3 convolution_bitcast_fusion.4
  281.7 1.6 fusion.13
  283.3 2.4 fusion.1
  285.7 2.5 divide_convert_fusion
  288.3 0.3 convolution_bitcast_fusion.3
  288.6 0.6 convolution_bitcast_fusion.5
  289.2 0.8 copy-done.1
  289.9 1.2 fusion.4
  291.2 0.5 copy.65
  291.7 0.1 reshape.453
  291.8 0.4 copy-done.4
  292.3 4.5 %collective-permute-start.3 = (bf16[1,1,64,1536]{3,2,1,0:T(8,128)(2,1)S(1)}, bf16[1,1,64,1536]{3,2,1,0:T(8,128)(2,1)S(1)}, u32[]{:S(2)}, u32[]{:S(2)}) collective-permute-start(bf16[1,1,64,1536]{3,2,1,0:T(8,128)(2,1)S(1)} %get-tuple-element.13), channel_id=1, source_target_pairs={{0,4},{4,8},{8,12},{12,16},{16,20},{20,24},{24,28},{1,5},{5,9},{9,... | collective-permute-start | bytes 589832 | tf_op jit(solution)/shard_map/ppermute | solution.py:21
  296.8 1.9 collective-permute-start.2
  298.7 0.6 collective-permute-done.3
  299.4 4.4 %collective-permute-done.2 = bf16[1,1,64,1536]{3,2,1,0:T(8,128)(2,1)S(1)} collective-permute-done((bf16[1,1,64,1536]{3,2,1,0:T(8,128)(2,1)S(1)}, bf16[1,1,64,1536]{3,2,1,0:T(8,128)(2,1)S(1)}, u32[]{:S(2)}, u32[]{:S(2)}) %collective-permute-start.2) | collective-permute-done | bytes 196640 | tf_op jit(solution)/shard_map/ppermute | solution.py:22
  303.8 0.2 multiply_reduce_fusion
  303.9 8.7 %psum.7 = f32[2,64]{1,0:T(2,128)S(1)} all-reduce(f32[2,64]{1,0:T(2,128)S(1)} %multiply_reduce_fusion), channel_id=1, replica_groups=mesh['dp'=32,'pipe'=8,'tensor'=4] {'tensor'}, use_global_device_ids=true, to_apply=%region_5.6 | all-reduce | flops 128 | bytes 1024 | tf_op jit(solution)/shard_map/psum | solution.py:141
  312.6 0.9 multiply_convert_fusion
  (52 shorter events, 1.7 us)
Async XLA Ops:
  3.8 50.5 %all-to-all-start = ((s32[32,1,2]{2,1,0:T(1,128)}), s32[32,1,2]{2,1,0:T(1,128)S(1)}, u32[]{:S(2)}, u32[]{:S(2)}) async-start(s32[32,1,2]{2,1,0:T(1,128)} %bitcast.14), calls=%async_computation | async-start | bytes 32768 | tf_op jit(solution)/shard_map/all_to_all | solution.py:81
  56.6 11.3 %copy-start.3 = (bf16[1,2,64,1536]{3,2,1,0:T(8,128)(2,1)S(1)}, bf16[1,2,64,1536]{3,2,1,0:T(8,128)(2,1)}, u32[]{:S(2)}) copy-start(bf16[1,2,64,1536]{3,2,1,0:T(8,128)(2,1)} %param.8) | copy-start | bytes 1179652
  56.6 220.2 %all-to-all-start.1 = ((bf16[32,2,2,64,128]{4,3,2,1,0:T(8,128)(2,1)}), bf16[32,2,2,64,128]{4,3,2,1,0:T(8,128)(2,1)}, u32[]{:S(2)}, u32[]{:S(2)}) async-start(bf16[32,2,2,64,128]{4,3,2,1,0:T(8,128)(2,1)} %bitcast.16), calls=%async_computation.1 | async-start | bytes 4194304 | tf_op jit(solution)/shard_map/all_to_all | solution.py:42
  61.5 198.1 %collective-permute-start.1 = (bf16[1,2,2,64,1536]{4,3,2,1,0:T(8,128)(2,1)}, bf16[1,2,2,64,1536]{4,3,2,1,0:T(8,128)(2,1)}, u32[]{:S(2)}, u32[]{:S(2)}) collective-permute-start(bf16[1,2,2,64,1536]{4,3,2,1,0:T(8,128)(2,1)} %param.9), channel_id=1, source_target_pairs={{32,0},{64,32},{96,64},{128,96},{160,128},{192,160},{224,192},{256... | collective-permute-start | bytes 2359304 | tf_op jit(solution)/shard_map/ppermute | solution.py:22
  62.8 196.8 %collective-permute-start = (bf16[1,2,2,64,1536]{4,3,2,1,0:T(8,128)(2,1)}, bf16[1,2,2,64,1536]{4,3,2,1,0:T(8,128)(2,1)}, u32[]{:S(2)}, u32[]{:S(2)}) collective-permute-start(bf16[1,2,2,64,1536]{4,3,2,1,0:T(8,128)(2,1)} %param.9), channel_id=1, source_target_pairs={{0,32},{32,64},{64,96},{96,128},{128,160},{160,192},{192,224},{224... | collective-permute-start | bytes 2359304 | tf_op jit(solution)/shard_map/ppermute | solution.py:21
  72.5 4.3 %copy-start.7 = (s32[1,2]{1,0:T(1,128)S(1)}, s32[1,2]{1,0:T(1,128)}, u32[]{:S(2)}) copy-start(s32[1,2]{1,0:T(1,128)} %param.12) | copy-start | bytes 28
  77.1 2.6 copy-start.5
  280.0 1.7 copy-start
  285.7 2.9 copy-start.2
  288.3 1.7 copy-start.1
  291.2 1.0 copy-start.4
  291.7 7.0 %copy-start.6 = (bf16[1,2,1536]{2,1,0:T(2,128)(2,1)S(1)}, bf16[1,2,1536]{2,1,0:T(2,128)(2,1)}, u32[]{:S(2)}) copy-start(bf16[1,2,1536]{2,1,0:T(2,128)(2,1)} %param.13) | copy-start | bytes 18436
  292.3 7.1 %collective-permute-start.3 = (bf16[1,1,64,1536]{3,2,1,0:T(8,128)(2,1)S(1)}, bf16[1,1,64,1536]{3,2,1,0:T(8,128)(2,1)S(1)}, u32[]{:S(2)}, u32[]{:S(2)}) collective-permute-start(bf16[1,1,64,1536]{3,2,1,0:T(8,128)(2,1)S(1)} %get-tuple-element.13), channel_id=1, source_target_pairs={{0,4},{4,8},{8,12},{12,16},{16,20},{20,24},{24,28},{1,5},{5,9},{9,... | collective-permute-start | bytes 589832 | tf_op jit(solution)/shard_map/ppermute | solution.py:21
  296.8 7.0 %collective-permute-start.2 = (bf16[1,1,64,1536]{3,2,1,0:T(8,128)(2,1)S(1)}, bf16[1,1,64,1536]{3,2,1,0:T(8,128)(2,1)S(1)}, u32[]{:S(2)}, u32[]{:S(2)}) collective-permute-start(bf16[1,1,64,1536]{3,2,1,0:T(8,128)(2,1)S(1)} %get-tuple-element.12), channel_id=1, source_target_pairs={{4,0},{8,4},{12,8},{16,12},{20,16},{24,20},{28,24},{5,1},{9,5},{13... | collective-permute-start | bytes 589832 | tf_op jit(solution)/shard_map/ppermute | solution.py:22
where the time goes:
time: 314 us
  waiting for transfers between devices  202 us (64%)
  starting transfers between devices  46.7 us (15%)
  local copies, waits for them, and re-layouts  36.1 us (11%)
  other arithmetic  11.8 us (4%)
  blocking collectives  8.71 us (3%)
  matrix products  8.08 us (3%)
    ppermute x2, waiting for transfers between devices, padded_2(): after = lax.ppermute(leading, axis, down)  182 us
    all_to_all x1, starting transfers between devices, body(): lax.all_to_all(wanted, 'dp', split_axis=0, concat_axis=0, tiled=True)  29.3 us
    all_to_all x1, waiting for transfers between devices, body(): lax.all_to_all(wanted, 'dp', split_axis=0, concat_axis=0, tiled=True)  19.3 us
    ppermute x2, starting transfers between devices, padded_2(): before = lax.ppermute(last, axis, up)  9.35 us
    psum x1, blocking collectives, body(): squares = lax.psum(jnp.sum(wide * wide, axis=2), 'tensor')  8.71 us
    unnamed x18, local copies, waits for them, and re-layouts  7.93 us
    another operation x3, local copies, waits for them, and re-layouts  7.19 us
  transfers between devices with their start and end apart: 6, of which 4 were waited for; matrix products, arithmetic and copies ran while one was open for 11% of the time, Pallas kernels for 0%

commit v1 on v0

v1 whole, which is shorter than its diff:
```python
import functools

import jax
import jax.numpy as jnp
from jax import lax
from jax.experimental import pallas as pl
from jax.experimental.pallas import tpu as pltpu
from jax.sharding import PartitionSpec as P

HD = 128
BLK = 64
EPSILON = 1e-05
REACH = 1
HIDDEN = 1e30
GROUP = 4
MESH = pl.DeviceIdType.MESH


def kernel(
    reach,
    ids,
    lens,
    res_hbm,
    q_hbm,
    kv_hbm,
    glob_hbm,
    gain_hbm,
    out,
    own,
    halo,
    q_v,
    glob_v,
    res_v,
    gain_v,
    want,
    table,
    table_s,
    send,
    send_half,
    recv,
    acc,
    row_max,
    row_sum,
    upd,
    squares,
    arrived,
    squares_in,
    own_sem,
    load_sem,
    want_sem,
    halo_send_sem,
    halo_recv_sem,
    tile_sem,
    tile_recv_sem,
    out_sem,
    in_sem,
):
    n = lax.axis_size("dp")
    sections = lax.axis_size("pipe")
    parts = lax.axis_size("tensor")
    me = lax.axis_index("dp")
    section = lax.axis_index("pipe")
    part = lax.axis_index("tensor")
    heads = q_v.shape[2] // HD
    group = GROUP if heads % GROUP == 0 else 1
    full = n // 2 - reach - 1
    scale = HD ** (-0.5)

    def ring(index):
        return lax.rem(index + 2 * n, n)

    def own_load(c, h):
        return pltpu.make_async_copy(
            kv_hbm.at[0, :, c, :, pl.ds(h * HD, HD)], own[c].at[h], own_sem.at[c, h]
        )

    loads = [
        pltpu.make_async_copy(q_hbm.at[0], q_v, load_sem.at[0]),
        pltpu.make_async_copy(glob_hbm.at[0], glob_v, load_sem.at[1]),
        pltpu.make_async_copy(res_hbm.at[0], res_v, load_sem.at[2]),
        pltpu.make_async_copy(gain_hbm.at[0], gain_v, load_sem.at[3]),
    ]
    for c in range(2):
        for h in range(heads):
            own_load(c, h).start()

    barrier = pltpu.get_barrier_semaphore()

    def greet(step, carry):
        pl.semaphore_signal(
            barrier, inc=1, device_id={"dp": ring(me + step)}, device_id_type=MESH
        )
        return carry

    lax.fori_loop(1, n, greet, 0)
    below = lax.rem(section + sections - 1, sections)
    above = lax.rem(section + 1, sections)
    for neighbour in (below, above):
        for peer in range(parts):
            pl.semaphore_signal(
                barrier,
                inc=1,
                device_id={"pipe": neighbour, "tensor": peer},
                device_id_type=MESH,
            )

    lane = lax.broadcasted_iota(jnp.int32, (1, 128), 1)
    row = jnp.zeros((1, 128), jnp.int32)
    for c in range(2):
        for h in range(heads):
            row = jnp.where(lane == ids[c, h] + c * n, h, row)
    want[...] = row
    table[0] = row

    pl.semaphore_wait(barrier, n - 1 + 2 * parts)

    def tell(step, carry):
        pltpu.make_async_remote_copy(
            src_ref=want,
            dst_ref=table.at[n - step],
            send_sem=want_sem.at[0],
            recv_sem=want_sem.at[1],
            device_id={"dp": ring(me + step)},
            device_id_type=MESH,
        ).start()
        return carry

    lax.fori_loop(1, n, tell, 0)

    def hop(direction, step, c):
        source = own[c] if step == 0 else halo[direction][step - 1][c]
        return pltpu.make_async_remote_copy(
            src_ref=source,
            dst_ref=halo[direction][step][c],
            send_sem=halo_send_sem.at[direction, step, c],
            recv_sem=halo_recv_sem.at[direction, step, c],
            device_id={"dp": ring(me + (1 if direction == 0 else -1))},
            device_id_type=MESH,
        )

    for c in range(2):
        for h in range(heads):
            own_load(c, h).wait()
        for direction in range(2):
            hop(direction, 0, c).start()
    for load in loads:
        load.start()

    rest = table.at[pl.ds(1, n - 1)]
    pltpu.make_async_copy(rest, rest, want_sem.at[1]).wait()
    to_smem = pltpu.make_async_copy(table, table_s, load_sem.at[4])
    to_smem.start()
    to_smem.wait()

    def push(source, destination, direction, distance, c, sem):
        pltpu.make_async_remote_copy(
            src_ref=source,
            dst_ref=destination,
            send_sem=tile_sem.at[sem],
            recv_sem=tile_recv_sem.at[c],
            device_id={"dp": ring(me + (1 - 2 * direction) * distance)},
            device_id_type=MESH,
        ).start()

    def serve(c):
        sources = [ring(me - reach), ring(me + reach)]

        def picked(direction, distance):
            asker = ring((1 - 2 * direction) * distance)
            return table_s[asker, 0, c * n + sources[direction]]

        for direction in range(2):
            head = picked(direction, full + 1)
            send_half[direction, c] = halo[direction][reach - 1][c][head][direction]
            push(
                send_half.at[direction, c],
                recv[c].at[sources[direction], direction],
                direction,
                full + 1,
                c,
                1,
            )

        def one(step, carry):
            distance = full - step
            for direction in range(2):
                head = picked(direction, distance)
                send[direction, c, distance - 1] = halo[direction][reach - 1][c][head]
                push(
                    send.at[direction, c, distance - 1],
                    recv[c].at[sources[direction]],
                    direction,
                    distance,
                    c,
                    0,
                )
            return carry

        lax.fori_loop(0, full, one, 0)

    for step in range(reach):
        for c in range(2):
            for direction in range(2):
                hop(direction, step, c).wait_recv()
                if step < reach - 1:
                    hop(direction, step + 1, c).start()
            if step == reach - 1:
                serve(c)

    for c in range(2):
        for offset in range(-reach, reach + 1):
            block = ring(me + offset)
            head = table_s[0, 0, c * n + block]
            if offset == 0:
                recv[c][block] = own[c][head]
            else:
                recv[c][block] = halo[int(offset > 0)][abs(offset) - 1][c][head]

    for load in loads:
        load.wait()

    def alive(block, live):
        return jnp.clip(live - block, 0, 1).astype(jnp.float32)

    def bias(valid):
        return (valid - 1.0) * HIDDEN

    def score(query, key):
        return (
            lax.dot_general(
                query, key, (((1,), (1,)), ((), ())), preferred_element_type=jnp.float32
            )
            * scale
        )

    def gather(weight, value):
        return jnp.dot(weight.astype(jnp.bfloat16), value, preferred_element_type=jnp.float32)

    for c in range(2):
        live = lens[c]
        bias_before = bias(alive(me - 1, live) * jnp.clip(me, 0, 1).astype(jnp.float32))
        bias_own = bias(alive(me, live))
        bias_after = bias(alive(me + 1, live))

        def near(step, carry):
            for k in range(group):
                h = step * group + k
                cols = pl.ds(pl.multiple_of(h * HD, HD), HD)
                query = q_v[c, :, cols]
                s_before = score(query, halo[0][0][c][h, 0]) + bias_before
                s_own = score(query, own[c][h, 0]) + bias_own
                s_after = score(query, halo[1][0][c][h, 0]) + bias_after
                s_glob = score(query, glob_v[0, c, :, cols])
                largest = jnp.max(jnp.maximum(jnp.maximum(s_before, s_own), s_after), axis=1, keepdims=True)
                largest = jnp.maximum(largest, jnp.max(s_glob, axis=1, keepdims=True))
                w_before = jnp.exp(s_before - largest)
                w_own = jnp.exp(s_own - largest)
                w_after = jnp.exp(s_after - largest)
                w_glob = jnp.exp(s_glob - largest)
                total = jnp.sum(w_before + w_own + w_after, axis=1, keepdims=True)
                total = total + jnp.sum(w_glob, axis=1, keepdims=True)
                context = gather(w_glob, glob_v[1, c, :, cols])
                context = context + gather(w_before, halo[0][0][c][h, 1])
                context = context + gather(w_own, own[c][h, 1])
                context = context + gather(w_after, halo[1][0][c][h, 1])
                acc[c, h] = context
                row_max[c, h] = jnp.broadcast_to(largest, (BLK, HD))
                row_sum[c, h] = jnp.broadcast_to(total, (BLK, HD))
            return carry

        lax.fori_loop(0, heads // group, near, 0)

    def stream_of(c):
        return pltpu.make_async_remote_copy(
            src_ref=upd.at[c],
            dst_ref=arrived.at[c],
            send_sem=out_sem.at[c, parts],
            recv_sem=in_sem.at[c, parts],
            device_id={"pipe": below if c == 0 else above},
            device_id_type=MESH,
        )

    def onward(c):
        target = below if c == 0 else above
        copies = [stream_of(c)]
        for peer in range(parts):
            copies.append(
                pltpu.make_async_remote_copy(
                    src_ref=squares.at[c],
                    dst_ref=squares_in.at[c, part],
                    send_sem=out_sem.at[c, peer],
                    recv_sem=in_sem.at[c, 0],
                    device_id={"pipe": target, "tensor": peer},
                    device_id_type=MESH,
                )
            )
        return copies

    for c in range(2):
        tiles = recv[c].at[pl.ds(0, n - 2 * reach - 1)]
        pltpu.make_async_copy(tiles, tiles, tile_recv_sem.at[c]).wait()
        live = lens[c]
        shown = alive(me, live)

        def far(step, total_squares):
            for k in range(group):
                h = step * group + k
                cols = pl.ds(pl.multiple_of(h * HD, HD), HD)
                block = ids[c, h]
                tile = recv[c][block]
                s_far = score(q_v[c, :, cols], tile[0]) + bias(alive(block, live))
                old = row_max[c, h]
                largest = jnp.maximum(old, jnp.max(s_far, axis=1, keepdims=True))
                shrink = jnp.exp(old - largest)
                w_far = jnp.exp(s_far - largest[:, :BLK])
                total = row_sum[c, h] * shrink + jnp.sum(w_far, axis=1, keepdims=True)
                context = (acc[c, h] * shrink + gather(w_far, tile[1])) / total
                state = res_v[c, :, cols].astype(jnp.float32) + context * shown
                state = state.astype(jnp.bfloat16)
                upd[c, :, cols] = state
                wide = state.astype(jnp.float32)
                total_squares = total_squares + wide * wide
            return total_squares

        squares[c] = lax.fori_loop(
            0, heads // group, far, jnp.zeros((BLK, HD), jnp.float32)
        )
        for copy in onward(c):
            copy.start()

    features = parts * heads * HD
    for c in range(2):
        stream_of(c).wait_recv()
        pltpu.make_async_copy(squares_in.at[c], squares_in.at[c], in_sem.at[c, 0]).wait()
        total = squares_in[c, 0]
        for peer in range(1, parts):
            total = total + squares_in[c, peer]
        inverse = lax.rsqrt(jnp.sum(total, axis=1, keepdims=True) / features + EPSILON)
        edge = section < sections - 1 if c == 0 else section > 0
        kept = jnp.where(edge, 1.0, 0.0).astype(jnp.float32)
        wide = arrived[c].astype(jnp.float32) * kept
        gains = gain_v[pl.ds(c, 1), :].astype(jnp.float32)
        out[c] = (wide * inverse * gains).astype(jnp.bfloat16)

    pltpu.make_async_copy(rest, rest, want_sem.at[0]).wait()
    pltpu.make_async_copy(send, send, tile_sem.at[0]).wait()
    pltpu.make_async_copy(send_half, send_half, tile_sem.at[1]).wait()
    for c in range(2):
        for step in range(reach):
            for direction in range(2):
                hop(direction, step, c).wait_send()
        for copy in onward(c):
            copy.wait_send()


def body(residual, queries, keys_values, global_kv, block_ids, lengths, gain):
    n = lax.axis_size("dp")
    parts = lax.axis_size("tensor")
    width = residual.shape[-1]
    heads = width // HD
    glob = global_kv.shape[3]
    reach = REACH
    full = n // 2 - reach - 1
    stream = (2, BLK, width)
    bf16, f32 = jnp.bfloat16, jnp.float32
    anywhere = pl.BlockSpec(memory_space=pl.ANY)
    scalars = pl.BlockSpec(memory_space=pltpu.SMEM)
    block = pltpu.VMEM((heads, 2, BLK, HD), bf16)
    normed = pl.pallas_call(
        functools.partial(kernel, reach),
        out_shape=jax.ShapeDtypeStruct(stream, bf16),
        in_specs=[scalars, scalars] + [anywhere] * 5,
        out_specs=pl.BlockSpec(memory_space=pltpu.VMEM),
        scratch_shapes=[
            [block] * 2,
            [[[block] * 2 for _ in range(reach)] for _ in range(2)],
            pltpu.VMEM(stream, bf16),
            pltpu.VMEM((2, 2, glob, width), bf16),
            pltpu.VMEM(stream, bf16),
            pltpu.VMEM((2, width), bf16),
            pltpu.VMEM((1, 128), jnp.int32),
            pltpu.VMEM((n, 1, 128), jnp.int32),
            pltpu.SMEM((n, 1, 128), jnp.int32),
            pltpu.VMEM((2, 2, full, 2, BLK, HD), bf16),
            pltpu.VMEM((2, 2, BLK, HD), bf16),
            [pltpu.VMEM((n, 2, BLK, HD), bf16)] * 2,
            pltpu.VMEM((2, heads, BLK, HD), f32),
            pltpu.VMEM((2, heads, BLK, HD), f32),
            pltpu.VMEM((2, heads, BLK, HD), f32),
            pltpu.VMEM(stream, bf16),
            pltpu.VMEM((2, BLK, HD), f32),
            pltpu.VMEM(stream, bf16),
            pltpu.VMEM((2, parts, BLK, HD), f32),
            pltpu.SemaphoreType.DMA((2, heads)),
            pltpu.SemaphoreType.DMA((5,)),
            pltpu.SemaphoreType.DMA((2,)),
            pltpu.SemaphoreType.DMA((2, reach, 2)),
            pltpu.SemaphoreType.DMA((2, reach, 2)),
            pltpu.SemaphoreType.DMA((2,)),
            pltpu.SemaphoreType.DMA((2,)),
            pltpu.SemaphoreType.DMA((2, parts + 1)),
            pltpu.SemaphoreType.DMA((2, parts + 1)),
        ],
        compiler_params=pltpu.CompilerParams(
            collective_id=0, has_side_effects=True, vmem_limit_bytes=48 << 20
        ),
        name="relay_step",
    )(
        block_ids.reshape(2, heads),
        lengths.reshape(2),
        residual,
        queries,
        keys_values,
        global_kv,
        gain,
    )
    return normed[None]


def solution(mesh):
    in_specs = (
        P("pipe", None, "dp", "tensor"),
        P("pipe", None, "dp", "tensor"),
        P("pipe", None, None, "dp", "tensor"),
        P("pipe", None, None, None, "tensor"),
        P("pipe", None, "dp", "tensor"),
        P("pipe", None),
        P("pipe", None, "tensor"),
    )
    out_specs = P("pipe", None, "dp", "tensor")
    return jax.shard_map(body, mesh=mesh, in_specs=in_specs, out_specs=out_specs, check_vma=False)
```

time: 314 us -> 224 us (0.71)
  Pallas kernels: 0 us -> 217 us
  waiting for transfers between devices: 202 us -> 0 us
  starting transfers between devices: 46.7 us -> 0 us
  local copies, waits for them, and re-layouts: 36.1 us -> 5.9 us
  other arithmetic: 11.8 us -> 0 us
  blocking collectives: 8.71 us -> 0 us
  matrix products: 8.08 us -> 0 us
    pallas_call x0 -> x1, Pallas kernels: none -> 217 us  [body(): pl.pallas_call(functools.partial(kernel, reach), out_shape=jax.ShapeDtype...]
    ppermute x4 -> x0, waiting for transfers between devices: 183 us -> none  [the longest x2 182 us: padded_2(): after = lax.ppermute(leading, axis, down)]
    all_to_all x2 -> x0, starting transfers between devices: 34.2 us -> none  [the longest x1 29.3 us: body(): lax.all_to_all(wanted, 'dp', split_axis=0, concat_axis=0, tiled=True)]
    all_to_all x2 -> x0, waiting for transfers between devices: 19.3 us -> none  [the longest x1 19.3 us: body(): lax.all_to_all(wanted, 'dp', split_axis=0, concat_axis=0, tiled=True)]
    ppermute x4 -> x0, starting transfers between devices: 12.6 us -> none  [the longest x2 9.35 us: padded_2(): before = lax.ppermute(last, axis, up)]
    another operation x5 -> x0, local copies, waits for them, and re-layouts: 8.97 us -> none
    slice x5 -> x0, local copies, waits for them, and re-layouts: 8.97 us -> none  [the longest x1 4.24 us: body(): global_pair[1]]
    psum x1 -> x0, blocking collectives: 8.71 us -> none  [body(): squares = lax.psum(jnp.sum(wide * wide, axis=2), 'tensor')]
  transfers between devices with their start and end apart: 6 -> 0, of which waited for: 4 -> 0; matrix products, arithmetic and copies ran while one was open for 11% -> 0% of each run, Pallas kernels for 0% -> 0%
where the time goes in v1:
time: 224 us; the launch traced here: 223 us
  Pallas kernels  217 us (97%)
  local copies, waits for them, and re-layouts  5.9 us (3%)
    pallas_call x1, Pallas kernels, body(): pl.pallas_call(functools.partial(kernel, reach), out_shape=jax.ShapeDtype...  217 us
    unnamed x13, local copies, waits for them, and re-layouts  5.9 us

profile of v1, /device:TPU:1, one launch (start us, length us, event | category | flops | bytes accessed | tf_op | source)
XLA Modules:
  0.0 222.6 jit_solution(15201907782465945752)
XLA Ops:
  0.0 0.0 copy-start
  0.0 1.1 copy-done
  1.1 0.0 copy-start.1
  1.1 1.0 copy-done.1
  2.1 0.0 copy-start.2
  2.1 1.0 copy-done.2
  3.1 0.0 copy-start.3
  3.1 0.7 copy-done.3
  3.8 0.0 copy-start.4
  3.8 0.7 copy-done.4
  4.5 0.0 copy-start.5
  4.5 0.7 copy-done.5
  5.2 216.7 %relay_step.1 = bf16[2,64,1536]{2,1,0:T(8,128)(2,1)S(1)} custom-call(s32[2,12]{1,0:T(2,128)S(1)} %bitcast.4, s32[2]{0:T(128)S(1)} %bitcast.5, bf16[1,2,64,1536]{3,2,1,0:T(8,128)(2,1)S(1)} %copy-done.1, bf16[1,2,64,1536]{3,2,1,0:T(8,128)(2,1)S(1)} %copy-done.2, bf16[1,2,2,64,1536]{4,3,2,1,0:T(8,128)(2,1)S(1)} %copy-done, ...), custom_call_target="tpu_custom_call" | custom-call | tf_op jit(solution)/shard_map/relay_step/pallas_call | solution.py:369
  221.9 0.7 copy.9
Async XLA Ops:
  0.0 1.1 copy-start
  1.1 1.0 copy-start.1
  2.1 1.0 copy-start.2
  3.1 0.7 copy-start.3
  3.8 0.7 copy-start.4
  4.5 0.7 copy-start.5

commit v2 on v1

--- a/solution.py
+++ b/solution.py
@@ -10,7 +10,7 @@
 HD = 128
 BLK = 64
 EPSILON = 1e-05
-REACH = 1
+REACH = 4
 HIDDEN = 1e30
 GROUP = 4
 MESH = pl.DeviceIdType.MESH
@@ -32,7 +32,6 @@
     glob_v,
     res_v,
     gain_v,
-    want,
     table,
     table_s,
     send,
@@ -47,7 +46,8 @@
     squares_in,
     own_sem,
     load_sem,
-    want_sem,
+    want_send_sem,
+    want_recv_sem,
     halo_send_sem,
     halo_recv_sem,
     tile_sem,
@@ -85,16 +85,12 @@
             own_load(c, h).start()
 
     barrier = pltpu.get_barrier_semaphore()
-
-    def greet(step, carry):
+    below = lax.rem(section + sections - 1, sections)
+    above = lax.rem(section + 1, sections)
+    for step in (1, n - 1):
         pl.semaphore_signal(
             barrier, inc=1, device_id={"dp": ring(me + step)}, device_id_type=MESH
         )
-        return carry
-
-    lax.fori_loop(1, n, greet, 0)
-    below = lax.rem(section + sections - 1, sections)
-    above = lax.rem(section + 1, sections)
     for neighbour in (below, above):
         for peer in range(parts):
             pl.semaphore_signal(
@@ -109,23 +105,30 @@
     for c in range(2):
         for h in range(heads):
             row = jnp.where(lane == ids[c, h] + c * n, h, row)
-    want[...] = row
-    table[0] = row
-
-    pl.semaphore_wait(barrier, n - 1 + 2 * parts)
-
-    def tell(step, carry):
-        pltpu.make_async_remote_copy(
-            src_ref=want,
-            dst_ref=table.at[n - step],
-            send_sem=want_sem.at[0],
-            recv_sem=want_sem.at[1],
-            device_id={"dp": ring(me + step)},
+    half = n // 2
+    table[half] = row
+
+    pl.semaphore_wait(barrier, 2 + 2 * parts)
+
+    rounds = half.bit_length() - 1
+
+    def spread(index, direction):
+        count = 1 << index
+        if direction == 0:
+            source, destination = half - count + 1, half - 2 * count + 1
+        else:
+            source, destination = half, half + count
+        return pltpu.make_async_remote_copy(
+            src_ref=table.at[pl.ds(source, count)],
+            dst_ref=table.at[pl.ds(destination, count)],
+            send_sem=want_send_sem.at[index, direction],
+            recv_sem=want_recv_sem.at[index, direction],
+            device_id={"dp": ring(me + (1 - 2 * direction) * count)},
             device_id_type=MESH,
-        ).start()
-        return carry
-
-    lax.fori_loop(1, n, tell, 0)
+        )
+
+    for direction in range(2):
+        spread(0, direction).start()
 
     def hop(direction, step, c):
         source = own[c] if step == 0 else halo[direction][step - 1][c]
@@ -146,12 +149,6 @@
     for load in loads:
         load.start()
 
-    rest = table.at[pl.ds(1, n - 1)]
-    pltpu.make_async_copy(rest, rest, want_sem.at[1]).wait()
-    to_smem = pltpu.make_async_copy(table, table_s, load_sem.at[4])
-    to_smem.start()
-    to_smem.wait()
-
     def push(source, destination, direction, distance, c, sem):
         pltpu.make_async_remote_copy(
             src_ref=source,
@@ -166,7 +163,7 @@
         sources = [ring(me - reach), ring(me + reach)]
 
         def picked(direction, distance):
-            asker = ring((1 - 2 * direction) * distance)
+            asker = half + (1 - 2 * direction) * distance
             return table_s[asker, 0, c * n + sources[direction]]
 
         for direction in range(2):
@@ -198,19 +195,40 @@
 
         lax.fori_loop(0, full, one, 0)
 
+    def advance(index):
+        for direction in range(2):
+            spread(index, direction).wait_recv()
+        if index < rounds - 1:
+            for direction in range(2):
+                spread(index + 1, direction).start()
+
+    to_come = list(range(rounds))
+    advance(to_come.pop(0))
     for step in range(reach):
         for c in range(2):
             for direction in range(2):
                 hop(direction, step, c).wait_recv()
                 if step < reach - 1:
                     hop(direction, step + 1, c).start()
-            if step == reach - 1:
-                serve(c)
+            if step < reach - 1:
+                if to_come:
+                    advance(to_come.pop(0))
+                continue
+            if c == 0:
+                while to_come:
+                    advance(to_come.pop(0))
+                rows = pl.ds(1, n - 1)
+                to_smem = pltpu.make_async_copy(
+                    table.at[rows], table_s.at[rows], load_sem.at[4]
+                )
+                to_smem.start()
+                to_smem.wait()
+            serve(c)
 
     for c in range(2):
         for offset in range(-reach, reach + 1):
             block = ring(me + offset)
-            head = table_s[0, 0, c * n + block]
+            head = table_s[half, 0, c * n + block]
             if offset == 0:
                 recv[c][block] = own[c][head]
             else:
@@ -322,8 +340,15 @@
                 total_squares = total_squares + wide * wide
             return total_squares
 
-        squares[c] = lax.fori_loop(
+        total_squares = lax.fori_loop(
             0, heads // group, far, jnp.zeros((BLK, HD), jnp.float32)
+        )
+        squares[c] = lax.dot_general(
+            jnp.ones((8, HD), jnp.float32),
+            jnp.concatenate([total_squares, total_squares], axis=0),
+            (((1,), (1,)), ((), ())),
+            precision=lax.Precision.HIGHEST,
+            preferred_element_type=jnp.float32,
         )
         for copy in onward(c):
             copy.start()
@@ -335,14 +360,23 @@
         total = squares_in[c, 0]
         for peer in range(1, parts):
             total = total + squares_in[c, peer]
-        inverse = lax.rsqrt(jnp.sum(total, axis=1, keepdims=True) / features + EPSILON)
+        mean = lax.dot_general(
+            total[:, :BLK],
+            jnp.full((8, HD), 1.0 / 8, jnp.float32),
+            (((0,), (0,)), ((), ())),
+            precision=lax.Precision.HIGHEST,
+            preferred_element_type=jnp.float32,
+        )
+        inverse = lax.rsqrt(mean[:, :1] / features + EPSILON)
         edge = section < sections - 1 if c == 0 else section > 0
         kept = jnp.where(edge, 1.0, 0.0).astype(jnp.float32)
         wide = arrived[c].astype(jnp.float32) * kept
         gains = gain_v[pl.ds(c, 1), :].astype(jnp.float32)
         out[c] = (wide * inverse * gains).astype(jnp.bfloat16)
 
-    pltpu.make_async_copy(rest, rest, want_sem.at[0]).wait()
+    for index in range(rounds):
+        for direction in range(2):
+            spread(index, direction).wait_send()
     pltpu.make_async_copy(send, send, tile_sem.at[0]).wait()
     pltpu.make_async_copy(send_half, send_half, tile_sem.at[1]).wait()
     for c in range(2):
@@ -361,15 +395,16 @@
     glob = global_kv.shape[3]
     reach = REACH
     full = n // 2 - reach - 1
+    rounds = (n // 2).bit_length() - 1
     stream = (2, BLK, width)
     bf16, f32 = jnp.bfloat16, jnp.float32
-    anywhere = pl.BlockSpec(memory_space=pl.ANY)
+    in_hbm = pl.BlockSpec(memory_space=pltpu.HBM)
     scalars = pl.BlockSpec(memory_space=pltpu.SMEM)
     block = pltpu.VMEM((heads, 2, BLK, HD), bf16)
     normed = pl.pallas_call(
         functools.partial(kernel, reach),
         out_shape=jax.ShapeDtypeStruct(stream, bf16),
-        in_specs=[scalars, scalars] + [anywhere] * 5,
+        in_specs=[scalars, scalars] + [in_hbm] * 5,
         out_specs=pl.BlockSpec(memory_space=pltpu.VMEM),
         scratch_shapes=[
             [block] * 2,
@@ -378,7 +413,6 @@
             pltpu.VMEM((2, 2, glob, width), bf16),
             pltpu.VMEM(stream, bf16),
             pltpu.VMEM((2, width), bf16),
-            pltpu.VMEM((1, 128), jnp.int32),
             pltpu.VMEM((n, 1, 128), jnp.int32),
             pltpu.SMEM((n, 1, 128), jnp.int32),
             pltpu.VMEM((2, 2, full, 2, BLK, HD), bf16),
@@ -388,12 +422,13 @@
             pltpu.VMEM((2, heads, BLK, HD), f32),
             pltpu.VMEM((2, heads, BLK, HD), f32),
             pltpu.VMEM(stream, bf16),
-            pltpu.VMEM((2, BLK, HD), f32),
+            pltpu.VMEM((2, 8, HD), f32),
             pltpu.VMEM(stream, bf16),
-            pltpu.VMEM((2, parts, BLK, HD), f32),
+            pltpu.VMEM((2, parts, 8, HD), f32),
             pltpu.SemaphoreType.DMA((2, heads)),
             pltpu.SemaphoreType.DMA((5,)),
-            pltpu.SemaphoreType.DMA((2,)),
+            pltpu.SemaphoreType.DMA((rounds, 2)),
+            pltpu.SemaphoreType.DMA((rounds, 2)),
             pltpu.SemaphoreType.DMA((2, reach, 2)),
             pltpu.SemaphoreType.DMA((2, reach, 2)),
             pltpu.SemaphoreType.DMA((2,)),
@@ -402,7 +437,7 @@
             pltpu.SemaphoreType.DMA((2, parts + 1)),
         ],
         compiler_params=pltpu.CompilerParams(
-            collective_id=0, has_side_effects=True, vmem_limit_bytes=48 << 20
+            collective_id=0, has_side_effects=True, vmem_limit_bytes=63 << 20
         ),
         name="relay_step",
     )(

time: 224 us -> 205 us (0.915)
  Pallas kernels: 217 us -> 202 us
  local copies, waits for them, and re-layouts: 5.9 us -> 1.77 us
    pallas_call x1, Pallas kernels: 217 us -> 202 us  [body(): pl.pallas_call(functools.partial(kernel, reach), out_shape=jax.ShapeDtype...]
    unnamed x13 -> x1, local copies, waits for them, and re-layouts: 5.9 us -> 1.77 us
where the time goes in v2:
time: 205 us; the launch traced here: 204 us
  Pallas kernels  202 us (99%)
    pallas_call x1, Pallas kernels, body(): pl.pallas_call(functools.partial(kernel, reach), out_shape=jax.ShapeDtype...  202 us

profile of v2, /device:TPU:1, one launch (start us, length us, event | category | flops | bytes accessed | tf_op | source)
XLA Modules:
  0.0 203.8 jit_solution(16236481542727973621)
XLA Ops:
  0.0 202.0 %relay_step.1 = bf16[2,64,1536]{2,1,0:T(8,128)(2,1)} custom-call(s32[2,12]{1,0:T(2,128)} %bitcast.4, s32[2]{0:T(128)} %bitcast.5, bf16[1,2,64,1536]{3,2,1,0:T(8,128)(2,1)} %res_hbm.1, bf16[1,2,64,1536]{3,2,1,0:T(8,128)(2,1)} %q_hbm.1, bf16[1,2,2,64,1536]{4,3,2,1,0:T(8,128)(2,1)} %kv_hbm.1, bf16[1,2,2,384,1536]{4,3,2,1,0:T(8,128)(2,1)} %glob_hbm.1, ...), custom_call_target="tpu_custom_call" | custom-call | tf_op jit(solution)/shard_map/relay_step/pallas_call | solution.py:404
  202.0 1.8 copy.9

commit v3 on v2

--- a/solution.py
+++ b/solution.py
@@ -52,8 +52,10 @@
     halo_recv_sem,
     tile_sem,
     tile_recv_sem,
-    out_sem,
-    in_sem,
+    stream_send_sem,
+    stream_recv_sem,
+    squares_send_sem,
+    squares_recv_sem,
 ):
     n = lax.axis_size("dp")
     sections = lax.axis_size("pipe")
@@ -203,16 +205,16 @@
                 spread(index + 1, direction).start()
 
     to_come = list(range(rounds))
-    advance(to_come.pop(0))
     for step in range(reach):
         for c in range(2):
-            for direction in range(2):
-                hop(direction, step, c).wait_recv()
-                if step < reach - 1:
-                    hop(direction, step + 1, c).start()
+            hop(0, step, c).wait_recv()
+            if c == 0 and to_come:
+                advance(to_come.pop(0))
             if step < reach - 1:
-                if to_come:
-                    advance(to_come.pop(0))
+                hop(0, step + 1, c).start()
+            hop(1, step, c).wait_recv()
+            if step < reach - 1:
+                hop(1, step + 1, c).start()
                 continue
             if c == 0:
                 while to_come:
@@ -288,31 +290,26 @@
 
         lax.fori_loop(0, heads // group, near, 0)
 
-    def stream_of(c):
+    def stream_of(c, step):
+        cols = pl.ds(pl.multiple_of(step * group * HD, HD), group * HD)
         return pltpu.make_async_remote_copy(
-            src_ref=upd.at[c],
-            dst_ref=arrived.at[c],
-            send_sem=out_sem.at[c, parts],
-            recv_sem=in_sem.at[c, parts],
+            src_ref=upd.at[c, :, cols],
+            dst_ref=arrived.at[c, :, cols],
+            send_sem=stream_send_sem.at[c, step],
+            recv_sem=stream_recv_sem.at[c, step],
             device_id={"pipe": below if c == 0 else above},
             device_id_type=MESH,
         )
 
-    def onward(c):
-        target = below if c == 0 else above
-        copies = [stream_of(c)]
-        for peer in range(parts):
-            copies.append(
-                pltpu.make_async_remote_copy(
-                    src_ref=squares.at[c],
-                    dst_ref=squares_in.at[c, part],
-                    send_sem=out_sem.at[c, peer],
-                    recv_sem=in_sem.at[c, 0],
-                    device_id={"pipe": target, "tensor": peer},
-                    device_id_type=MESH,
-                )
-            )
-        return copies
+    def squares_of(c, peer):
+        return pltpu.make_async_remote_copy(
+            src_ref=squares.at[c],
+            dst_ref=squares_in.at[c, part],
+            send_sem=squares_send_sem.at[c, peer],
+            recv_sem=squares_recv_sem.at[c],
+            device_id={"pipe": below if c == 0 else above, "tensor": peer},
+            device_id_type=MESH,
+        )
 
     for c in range(2):
         tiles = recv[c].at[pl.ds(0, n - 2 * reach - 1)]
@@ -338,6 +335,7 @@
                 upd[c, :, cols] = state
                 wide = state.astype(jnp.float32)
                 total_squares = total_squares + wide * wide
+            stream_of(c, step).start()
             return total_squares
 
         total_squares = lax.fori_loop(
@@ -350,13 +348,14 @@
             precision=lax.Precision.HIGHEST,
             preferred_element_type=jnp.float32,
         )
-        for copy in onward(c):
-            copy.start()
+        for peer in range(parts):
+            squares_of(c, peer).start()
 
     features = parts * heads * HD
     for c in range(2):
-        stream_of(c).wait_recv()
-        pltpu.make_async_copy(squares_in.at[c], squares_in.at[c], in_sem.at[c, 0]).wait()
+        for step in range(heads // group):
+            stream_of(c, step).wait_recv()
+        pltpu.make_async_copy(squares_in.at[c], squares_in.at[c], squares_recv_sem.at[c]).wait()
         total = squares_in[c, 0]
         for peer in range(1, parts):
             total = total + squares_in[c, peer]
@@ -383,8 +382,10 @@
         for step in range(reach):
             for direction in range(2):
                 hop(direction, step, c).wait_send()
-        for copy in onward(c):
-            copy.wait_send()
+        for step in range(heads // group):
+            stream_of(c, step).wait_send()
+        for peer in range(parts):
+            squares_of(c, peer).wait_send()
 
 
 def body(residual, queries, keys_values, global_kv, block_ids, lengths, gain):
@@ -433,8 +434,10 @@
             pltpu.SemaphoreType.DMA((2, reach, 2)),
             pltpu.SemaphoreType.DMA((2,)),
             pltpu.SemaphoreType.DMA((2,)),
-            pltpu.SemaphoreType.DMA((2, parts + 1)),
-            pltpu.SemaphoreType.DMA((2, parts + 1)),
+            pltpu.SemaphoreType.DMA((2, heads)),
+            pltpu.SemaphoreType.DMA((2, heads)),
+            pltpu.SemaphoreType.DMA((2, parts)),
+            pltpu.SemaphoreType.DMA((2,)),
         ],
         compiler_params=pltpu.CompilerParams(
             collective_id=0, has_side_effects=True, vmem_limit_bytes=63 << 20

time: 205 us -> 205 us (level)
  no operation moved by 1% of the time
where the time goes in v3:
time: 205 us; the launch traced here: 204 us
  Pallas kernels  203 us (99%)
    pallas_call x1, Pallas kernels, body(): pl.pallas_call(functools.partial(kernel, reach), out_shape=jax.ShapeDtype...  203 us

profile of v3, /device:TPU:1, one launch (start us, length us, event | category | flops | bytes accessed | tf_op | source)
XLA Modules:
  0.0 204.4 jit_solution(6525739990775471038)
XLA Ops:
  0.0 202.6 %relay_step.1 = bf16[2,64,1536]{2,1,0:T(8,128)(2,1)} custom-call(s32[2,12]{1,0:T(2,128)} %bitcast.4, s32[2]{0:T(128)} %bitcast.5, bf16[1,2,64,1536]{3,2,1,0:T(8,128)(2,1)} %res_hbm.1, bf16[1,2,64,1536]{3,2,1,0:T(8,128)(2,1)} %q_hbm.1, bf16[1,2,2,64,1536]{4,3,2,1,0:T(8,128)(2,1)} %kv_hbm.1, bf16[1,2,2,384,1536]{4,3,2,1,0:T(8,128)(2,1)} %glob_hbm.1, ...), custom_call_target="tpu_custom_call" | custom-call | tf_op jit(solution)/shard_map/relay_step/pallas_call | solution.py:405
  202.6 1.8 copy.9
